TPU v7x, 32 devices: a whole 2x2x4 slice. The times are simulated.
32 devices in a mesh: dp: 8 (over z, x), tensor: 4 (over y, core).
Axes of the slice: x: 2, y: 2, z: 4, core: 2. Of those that a mesh axis runs over, the one named last changes fastest.
Arguments:
- inputs: bfloat16 [16384, 768], P(('dp', 'tensor')), may hold values from -6 to 6
- teacher: bfloat16 [16384, 768], P(('dp', 'tensor')), may hold values from -6 to 6
- lengths: int32 [8], P('dp'), may hold values from 512 to 2048
- buckets: int32 [4096], replicated, may hold values from 0 to 31
- gain_attn: bfloat16 [768], replicated, may hold values from 0.25 to 1.75
- w_query: bfloat16 [768, 768], P(None, 'tensor'), may hold values from -0.4375 to 0.4375
- w_key: bfloat16 [768, 768], P(None, 'tensor'), may hold values from -0.21875 to 0.21875
- w_value: bfloat16 [768, 768], P(None, 'tensor'), may hold values from -0.21875 to 0.21875
- w_out: bfloat16 [768, 768], P('tensor'), may hold values from -1.75 to 1.75
- bias_table: bfloat16 [32, 12], P(None, 'tensor'), may hold values from -4 to 4
- gain_ff: bfloat16 [768], replicated, may hold values from 0.25 to 1.75
- w_gate: bfloat16 [768, 2048], P(None, 'tensor'), may hold values from -0.21875 to 0.21875
- w_up: bfloat16 [768, 2048], P(None, 'tensor'), may hold values from -0.21875 to 0.21875
- w_down: bfloat16 [2048, 768], P('tensor'), may hold values from -0.125 to 0.125
Outputs:
- activations: bfloat16 [16384, 768], P(('dp', 'tensor'))
- loss: float32 [], replicated
- grad_inputs: float32 [16384, 768], P(('dp', 'tensor'))
- grad_gain_attn: float32 [768], replicated
- grad_query: float32 [768, 768], P(None, 'tensor')
- grad_key: float32 [768, 768], P(None, 'tensor')
- grad_value: float32 [768, 768], P(None, 'tensor')
- grad_out: float32 [768, 768], P('tensor')
- grad_table: float32 [32, 12], P(None, 'tensor')
- grad_gain_ff: float32 [768], replicated
- grad_gate: float32 [768, 2048], P(None, 'tensor')
- grad_up: float32 [768, 2048], P(None, 'tensor')
- grad_down: float32 [2048, 768], P('tensor')
All inputs are finite; a program needn't handle non-finite values.
Results may differ from a plain program's by a relative error of at most 0.015.
The roundings to bfloat16 on the way count: a program that leaves them out, or rounds other values in their place, can miss the bound.
Values may be sent and summed in bfloat16 or wider, within the bound.
A program may use at most 320 MiB of HBM per device.

v0:
```python
import jax
import jax.numpy as jnp
from jax import lax
from jax.sharding import PartitionSpec as P

QBLOCK = 512
eps_norm = 1e-06
masked_score = -1e30
highest = lax.Precision.HIGHEST
contract_rows = (((0,), (0,)), ((), ()))
contract_cols = (((1,), (1,)), ((), ()))
contract_table = (((0,), (1,)), ((), ()))


def row_norm(values, gain):
    inverse = lax.rsqrt(jnp.mean(values * values, axis=-1, keepdims=True) + eps_norm)
    return values * inverse * gain


def geglu_mask(gate_values, up_values, keep_column):
    return keep_column * jax.nn.gelu(gate_values, approximate=True) * up_values


def valid_mask(lengths, first_row, row_count, seq_len):
    positions = first_row + lax.iota(jnp.int32, row_count)
    owners = positions // seq_len
    within = positions % seq_len
    chosen = owners[:, None] == lax.iota(jnp.int32, lengths.shape[0])[None, :]
    limits = jnp.sum(jnp.where(chosen, lengths[None, :], 0), axis=1)
    return (within < limits).astype(jnp.float32)


def bucket_rows(buckets, bias_table):
    one_hot = (buckets[:, None] == lax.iota(jnp.int32, bias_table.shape[0])[None, :]).astype(
        jnp.float32
    )
    relative = lax.dot_general(
        bias_table.astype(jnp.float32), one_hot, contract_table, precision=highest
    )
    return (one_hot, relative)


def band_matrix(window, block_rows, seq_len):
    heads_here = window.shape[0]
    span = seq_len + block_rows - 1
    tiled = jnp.tile(window, (1, block_rows + 1))
    tiled = tiled[:, block_rows - 1 : block_rows - 1 + block_rows * (span - 1)]
    return tiled.reshape(heads_here, block_rows, span - 1)[:, :, :seq_len]


def make_bands(relative, block_rows, seq_len):
    pieces = []
    for block_index in range(seq_len // block_rows):
        first_row = block_index * block_rows
        start = seq_len - first_row - block_rows + 1
        window = relative[:, start : start + seq_len + block_rows - 1]
        pieces.append(band_matrix(window, block_rows, seq_len))
    return jnp.stack(pieces, axis=1)


def attend_head(query_head, key_head, value_head, keep_seq, length, bands_head, block_rows, scale):
    seq_len, head_dim = query_head.shape
    key_live = lax.iota(jnp.int32, seq_len) < length

    def one_block(step_index, totals):
        mixed_rows, log_sums = totals
        first_row = step_index * block_rows
        query_block = lax.dynamic_slice_in_dim(query_head, first_row, block_rows, 0)
        band = lax.dynamic_index_in_dim(bands_head, step_index, 0, keepdims=False)
        raw_scores = lax.dot_general(
            query_block, key_head, contract_cols, preferred_element_type=jnp.float32
        )
        scores = jnp.where(key_live[None, :], raw_scores * scale + band, masked_score)
        row_max = jnp.max(scores, axis=-1, keepdims=True)
        expos = jnp.exp(scores - row_max)
        row_total = jnp.sum(expos, axis=-1, keepdims=True)
        probs = (expos / row_total).astype(jnp.bfloat16)
        mixed = jnp.dot(probs, value_head, preferred_element_type=jnp.float32)
        keep_block = lax.dynamic_slice_in_dim(keep_seq, first_row, block_rows, 0)
        mixed = (mixed * keep_block[:, None]).astype(jnp.bfloat16)
        mixed_rows = lax.dynamic_update_slice_in_dim(mixed_rows, mixed, first_row, 0)
        log_sums = lax.dynamic_update_slice_in_dim(
            log_sums, (row_max + jnp.log(row_total))[:, 0], first_row, 0
        )
        return (mixed_rows, log_sums)

    initial = (jnp.zeros((seq_len, head_dim), jnp.bfloat16), jnp.zeros((seq_len,), jnp.float32))
    return lax.fori_loop(0, seq_len // block_rows, one_block, initial)


def attend_head_back(
    query_head,
    key_head,
    value_head,
    grad_head,
    log_sums,
    length,
    bands_head,
    grad_bands_head,
    block_rows,
    scale,
):
    seq_len, head_dim = query_head.shape
    key_live = lax.iota(jnp.int32, seq_len) < length

    def one_block(step_index, totals):
        grad_query, grad_key, grad_value, grad_band = totals
        first_row = step_index * block_rows
        query_block = lax.dynamic_slice_in_dim(query_head, first_row, block_rows, 0)
        grad_block = lax.dynamic_slice_in_dim(grad_head, first_row, block_rows, 0)
        band = lax.dynamic_index_in_dim(bands_head, step_index, 0, keepdims=False)
        raw_scores = lax.dot_general(
            query_block, key_head, contract_cols, preferred_element_type=jnp.float32
        )
        scores = jnp.where(key_live[None, :], raw_scores * scale + band, masked_score)
        block_sums = lax.dynamic_slice_in_dim(log_sums, first_row, block_rows, 0)
        probs = jnp.exp(scores - block_sums[:, None])
        grad_value = grad_value + lax.dot_general(
            probs.astype(jnp.bfloat16),
            grad_block,
            contract_rows,
            preferred_element_type=jnp.float32,
        )
        grad_probs = lax.dot_general(
            grad_block, value_head, contract_cols, preferred_element_type=jnp.float32
        )
        inner = jnp.sum(probs * grad_probs, axis=-1, keepdims=True)
        grad_scores = (probs * (grad_probs - inner)).astype(jnp.bfloat16)
        grad_query_block = (
            jnp.dot(grad_scores, key_head, preferred_element_type=jnp.float32) * scale
        )
        grad_query = lax.dynamic_update_slice_in_dim(
            grad_query, grad_query_block.astype(jnp.bfloat16), first_row, 0
        )
        grad_key = (
            grad_key
            + lax.dot_general(
                grad_scores, query_block, contract_rows, preferred_element_type=jnp.float32
            )
            * scale
        )
        current = lax.dynamic_index_in_dim(grad_band, step_index, 0, keepdims=True)
        grad_band = lax.dynamic_update_slice_in_dim(
            grad_band, current + grad_scores.astype(jnp.float32)[None], step_index, 0
        )
        return (grad_query, grad_key, grad_value, grad_band)

    initial = (
        jnp.zeros((seq_len, head_dim), jnp.bfloat16),
        jnp.zeros((seq_len, head_dim), jnp.float32),
        jnp.zeros((seq_len, head_dim), jnp.float32),
        grad_bands_head,
    )
    return lax.fori_loop(0, seq_len // block_rows, one_block, initial)


def on_device(
    inputs,
    teacher,
    lengths,
    buckets,
    gain_attn,
    w_query,
    w_key,
    w_value,
    w_out,
    bias_table,
    gain_ff,
    w_gate,
    w_up,
    w_down,
):
    row_count, model_width = inputs.shape
    group_size = lax.axis_size("tensor")
    seq_len = buckets.shape[0] // 2
    all_rows = row_count * group_size
    block_rows = QBLOCK
    local_width = w_query.shape[1]
    heads_here = bias_table.shape[1]
    head_dim = local_width // heads_here
    ff_width = w_gate.shape[1]
    scale = head_dim ** (-0.5)
    my_first = lax.axis_index("tensor") * row_count
    keep_mine = valid_mask(lengths, my_first, row_count, seq_len)
    keep_all = valid_mask(lengths, 0, all_rows, seq_len)
    one_hot, relative = bucket_rows(buckets, bias_table)
    bands = make_bands(relative, block_rows, seq_len)
    gain_a = gain_attn.astype(jnp.float32)
    gain_f = gain_ff.astype(jnp.float32)
    source = inputs.astype(jnp.float32)
    normed = row_norm(source, gain_a).astype(jnp.bfloat16)
    normed_all = lax.all_gather(normed, "tensor", axis=0, tiled=True)
    w_joint = jnp.concatenate([w_query, w_key, w_value], axis=1)

    def head_proj(weight, head):
        columns = weight[:, head * head_dim : (head + 1) * head_dim]
        return jnp.dot(normed_all, columns, preferred_element_type=jnp.float32).astype(jnp.bfloat16)

    query_heads = [head_proj(w_query, head) for head in range(heads_here)]
    key_heads = [head_proj(w_key, head) for head in range(heads_here)]
    value_heads = [head_proj(w_value, head) for head in range(heads_here)]
    seq_index = 0
    head_mixed = []
    head_sums = []
    for head in range(heads_here):
        mixed_head, sums_head = attend_head(
            query_heads[head],
            key_heads[head],
            value_heads[head],
            keep_all,
            lengths[seq_index],
            bands[head],
            block_rows,
            scale,
        )
        head_mixed.append(mixed_head)
        head_sums.append(sums_head)
    mixed_parts = jnp.concatenate(head_mixed, axis=1)
    sums_parts = [head_sums]
    middle = source + lax.psum_scatter(
        jnp.dot(mixed_parts, w_out, preferred_element_type=jnp.float32).astype(jnp.bfloat16),
        "tensor",
        scatter_dimension=0,
        tiled=True,
    ).astype(jnp.float32)
    normed_ff = row_norm(middle, gain_f).astype(jnp.bfloat16)
    normed_ff_all = lax.all_gather(normed_ff, "tensor", axis=0, tiled=True)
    w_pair = jnp.concatenate([w_gate, w_up], axis=1)
    paired = jnp.dot(normed_ff_all, w_pair, preferred_element_type=jnp.float32)
    gate_values = paired[:, :ff_width]
    up_values = paired[:, ff_width:]
    hidden = geglu_mask(gate_values, up_values, keep_all[:, None]).astype(jnp.bfloat16)
    output = middle + lax.psum_scatter(
        jnp.dot(hidden, w_down, preferred_element_type=jnp.float32).astype(jnp.bfloat16),
        "tensor",
        scatter_dimension=0,
        tiled=True,
    ).astype(jnp.float32)
    activations = output.astype(jnp.bfloat16)
    cotangent = keep_mine[:, None] * (output - teacher.astype(jnp.float32))
    loss_part = jnp.sum(cotangent * cotangent)
    count_part = jnp.sum(keep_mine)
    shard_piece = lax.all_gather(cotangent.astype(jnp.bfloat16), "tensor", axis=0, tiled=True)
    grad_down_acc = lax.dot_general(
        hidden, shard_piece, contract_rows, preferred_element_type=jnp.float32
    )
    grad_rows = lax.dot_general(
        shard_piece, w_down, contract_cols, preferred_element_type=jnp.float32
    )
    grad_down = grad_down_acc
    grad_hidden = grad_rows
    _, geglu_back = jax.vjp(
        lambda gate_in, up_in: geglu_mask(gate_in, up_in, keep_all[:, None]), gate_values, up_values
    )
    grad_gate_rows, grad_up_rows = geglu_back(grad_hidden)
    grad_pair = jnp.concatenate([grad_gate_rows, grad_up_rows], axis=1).astype(jnp.bfloat16)
    grad_w_pair = lax.dot_general(
        normed_ff_all, grad_pair, contract_rows, preferred_element_type=jnp.float32
    )
    grad_normed_ff = lax.psum_scatter(
        lax.dot_general(
            grad_pair, w_pair, contract_cols, preferred_element_type=jnp.float32
        ).astype(jnp.bfloat16),
        "tensor",
        scatter_dimension=0,
        tiled=True,
    ).astype(jnp.float32)
    _, norm_back_ff = jax.vjp(row_norm, middle, gain_f)
    grad_middle_part, grad_gain_ff = norm_back_ff(grad_normed_ff)
    grad_middle = cotangent + grad_middle_part
    shard_piece = lax.all_gather(grad_middle.astype(jnp.bfloat16), "tensor", axis=0, tiled=True)
    grad_out_acc = lax.dot_general(
        mixed_parts, shard_piece, contract_rows, preferred_element_type=jnp.float32
    )
    grad_rows = lax.dot_general(
        shard_piece, w_out, contract_cols, preferred_element_type=jnp.float32
    )
    grad_out = grad_out_acc
    grad_mix = grad_rows.astype(jnp.bfloat16) * keep_all[:, None].astype(jnp.bfloat16)
    grad_bands = [jnp.zeros(bands.shape[1:], jnp.float32) for head in range(heads_here)]
    seq_index = 0
    low_row = seq_index * seq_len
    query_grads = []
    key_grads = []
    value_grads = []
    for head in range(heads_here):
        grad_head = grad_mix[low_row : low_row + seq_len, head * head_dim : (head + 1) * head_dim]
        grad_q, grad_k, grad_v, grad_bands[head] = attend_head_back(
            query_heads[head],
            key_heads[head],
            value_heads[head],
            grad_head,
            sums_parts[seq_index][head],
            lengths[seq_index],
            bands[head],
            grad_bands[head],
            block_rows,
            scale,
        )
        query_grads.append(grad_q)
        key_grads.append(grad_k.astype(jnp.bfloat16))
        value_grads.append(grad_v.astype(jnp.bfloat16))
    grad_parts = jnp.concatenate(query_grads + key_grads + value_grads, axis=1)
    _, bands_back = jax.vjp(lambda values: make_bands(values, block_rows, seq_len), relative)
    (grad_relative,) = bands_back(jnp.stack(grad_bands, axis=0))
    grad_w_joint = lax.dot_general(
        normed_all, grad_parts, contract_rows, preferred_element_type=jnp.float32
    )
    grad_table = lax.dot_general(one_hot, grad_relative, contract_table, precision=highest)
    grad_normed = lax.psum_scatter(
        lax.dot_general(
            grad_parts, w_joint, contract_cols, preferred_element_type=jnp.float32
        ).astype(jnp.bfloat16),
        "tensor",
        scatter_dimension=0,
        tiled=True,
    ).astype(jnp.float32)
    _, norm_back_attn = jax.vjp(row_norm, source, gain_a)
    grad_source_part, grad_gain_attn = norm_back_attn(grad_normed)
    grad_source = grad_middle + grad_source_part
    gain_attn_total, gain_ff_total, loss_total, count_total = lax.psum(
        (grad_gain_attn, grad_gain_ff, loss_part, count_part), ("dp", "tensor")
    )
    grad_w_joint, grad_out, grad_table, grad_w_pair, grad_down = lax.psum(
        (grad_w_joint, grad_out, grad_table, grad_w_pair, grad_down), "dp"
    )
    factor = 2.0 / (count_total * model_width)
    loss = loss_total / (count_total * model_width)
    return (
        activations,
        loss,
        grad_source * factor,
        gain_attn_total * factor,
        grad_w_joint[:, :local_width] * factor,
        grad_w_joint[:, local_width : 2 * local_width] * factor,
        grad_w_joint[:, 2 * local_width :] * factor,
        grad_out * factor,
        grad_table * factor,
        gain_ff_total * factor,
        grad_w_pair[:, :ff_width] * factor,
        grad_w_pair[:, ff_width:] * factor,
        grad_down * factor,
    )


def solution(mesh):
    in_specs = (
        P(("dp", "tensor"), None),
        P(("dp", "tensor"), None),
        P("dp"),
        P(),
        P(),
        P(None, "tensor"),
        P(None, "tensor"),
        P(None, "tensor"),
        P("tensor", None),
        P(None, "tensor"),
        P(),
        P(None, "tensor"),
        P(None, "tensor"),
        P("tensor", None),
    )
    out_specs = (
        P(("dp", "tensor"), None),
        P(),
        P(("dp", "tensor"), None),
        P(),
        P(None, "tensor"),
        P(None, "tensor"),
        P(None, "tensor"),
        P("tensor", None),
        P(None, "tensor"),
        P(),
        P(None, "tensor"),
        P(None, "tensor"),
        P("tensor", None),
    )
    return jax.shard_map(
        on_device, mesh=mesh, in_specs=in_specs, out_specs=out_specs, check_vma=False
    )
```

profile of v0, /device:TPU:12, one launch (start us, length us, event | category | flops | bytes accessed | tf_op | source)
XLA Modules:
  0.0 2143.7 jit_solution(9181588129690975066)
XLA Ops:
  22.7 24.2 %reshape.252 = f32[3938301]{0:T(1024)} reshape(f32[3,513,2559]{2,1,0:T(8,128)} %tile.40) | data formatting | bytes 31506408
  46.9 23.7 %tile.41 = f32[3,1312767]{1,0:T(4,128)} reshape(f32[3938301]{0:T(1024)} %reshape.252) | data formatting | bytes 31506408 | tf_op jit(solution)/shard_map/tile | solution.py:46
  92.4 44.4 %reshape.254 = f32[3929088]{0:T(1024)} reshape(f32[3,1309696]{1,0:T(4,128)} %slice.146) | data formatting | bytes 31432704
  136.8 24.7 %reshape.232 = f32[3,512,2558]{2,1,0:T(8,128)} reshape(f32[3929088]{0:T(1024)} %reshape.254) | data formatting | bytes 31432704 | tf_op jit(solution)/shard_map/reshape | solution.py:48
  169.1 24.2 %reshape.248 = f32[3938301]{0:T(1024)} reshape(f32[3,513,2559]{2,1,0:T(8,128)} %tile.42) | data formatting | bytes 31506408
  193.2 23.7 %tile.43 = f32[3,1312767]{1,0:T(4,128)} reshape(f32[3938301]{0:T(1024)} %reshape.248) | data formatting | bytes 31506408 | tf_op jit(solution)/shard_map/tile | solution.py:46
  238.5 44.7 %reshape.250 = f32[3929088]{0:T(1024)} reshape(f32[3,1309696]{1,0:T(4,128)} %slice.149) | data formatting | bytes 31432704
  283.2 24.8 %reshape.233 = f32[3,512,2558]{2,1,0:T(8,128)} reshape(f32[3929088]{0:T(1024)} %reshape.250) | data formatting | bytes 31432704 | tf_op jit(solution)/shard_map/reshape | solution.py:48
  315.5 23.9 %reshape.260 = f32[3938301]{0:T(1024)} reshape(f32[3,513,2559]{2,1,0:T(8,128)} %tile.16) | data formatting | bytes 31506408
  339.5 23.7 %tile.17 = f32[3,1312767]{1,0:T(4,128)} reshape(f32[3938301]{0:T(1024)} %reshape.260) | data formatting | bytes 31506408 | tf_op jit(solution)/shard_map/tile | solution.py:46
  385.0 44.4 %reshape.262 = f32[3929088]{0:T(1024)} reshape(f32[3,1309696]{1,0:T(4,128)} %slice.140) | data formatting | bytes 31432704
  429.5 24.8 %reshape.230 = f32[3,512,2558]{2,1,0:T(8,128)} reshape(f32[3929088]{0:T(1024)} %reshape.262) | data formatting | bytes 31432704 | tf_op jit(solution)/shard_map/reshape | solution.py:48
  461.8 24.2 %reshape.256 = f32[3938301]{0:T(1024)} reshape(f32[3,513,2559]{2,1,0:T(8,128)} %tile.18) | data formatting | bytes 31506408
  485.9 23.7 %tile.19 = f32[3,1312767]{1,0:T(4,128)} reshape(f32[3938301]{0:T(1024)} %reshape.256) | data formatting | bytes 31506408 | tf_op jit(solution)/shard_map/tile | solution.py:46
  531.3 44.7 %reshape.258 = f32[3929088]{0:T(1024)} reshape(f32[3,1309696]{1,0:T(4,128)} %slice.143) | data formatting | bytes 31432704
  575.9 24.8 %reshape.231 = f32[3,512,2558]{2,1,0:T(8,128)} reshape(f32[3929088]{0:T(1024)} %reshape.258) | data formatting | bytes 31432704 | tf_op jit(solution)/shard_map/reshape | solution.py:48
  635.3 34.5 %pad_maximum_fusion = f32[3,4,512,2048]{3,2,1,0:T(8,128)} fusion(f32[3,1,512,2048]{3,2,1,0:T(8,128)} %get-tuple-element.1597, f32[3,1,512,2048]{3,2,1,0:T(8,128)} %get-tuple-element.1598, f32[3,1,512,2048]{3,2,1,0:T(8,128)} %get-tuple-element.1599, f32[3,1,512,2048]{3,2,1,0:T(8,128)} %get-tuple-element.1600), kind=kLoop, calls=%fused_computation.120 | loop fusion | flops 37748736 | bytes 100663296 | tf_op jit(solution)/shard_map/stack | solution.py:58
  669.8 33.4 %slice_bitcast_fusion = (f32[4,512,2048]{2,1,0:T(8,128)}, f32[4,512,2048]{2,1,0:T(8,128)}, f32[4,512,2048]{2,1,0:T(8,128)}) fusion(f32[3,4,512,2048]{3,2,1,0:T(8,128)} %pad_maximum_fusion), kind=kLoop, calls=%fused_computation.122 | loop fusion | bytes 100663296 | tf_op jit(solution)/shard_map/squeeze | solution.py:212
  715.0 31.0 %while.109 = (s32[]{:T(128)}, bf16[2048,64]{0,1:T(8,128)(2,1)}, f32[2048]{0:T(1024)}, bf16[2048,64]{1,0:T(8,128)(2,1)}, bf16[2048,64]{1,0:T(8,128)(2,1)S(1)}, /*...) while((s32[]{:T(128)}, bf16[2048,64]{0,1:T(8,128)(2,1)}, ...), condition=%wide.region_8.9_spmd.clone, body=%wide.region_5.8_spmd.clone.sunk | while | flops 277939712 | bytes 17525440 | solution.py:88
  756.9 23.2 %while.108 = (s32[]{:T(128)}, bf16[2048,64]{0,1:T(8,128)(2,1)S(1)}, f32[2048]{0:T(1024)S(1)}, bf16[2048,64]{1,0:T(8,128)(2,1)}, bf16[2048,64]{1,0:T(8,128)(2,1)S...) while((s32[]{:T(128)}, bf16[2048,64]{0,1:T(8,128)(2,1)S(1)}, ...), condition=%wide.region_4.5_spmd.clone, body=%wide.region_1.4_spmd.clone.sunk | while | flops 277939712 | bytes 17787584 | solution.py:88
  792.2 27.5 %while.110 = (s32[]{:T(128)}, bf16[2048,64]{0,1:T(8,128)(2,1)S(1)}, f32[2048]{0:T(1024)S(1)}, bf16[2048,64]{1,0:T(8,128)(2,1)}, bf16[2048,64]{1,0:T(8,128)(2,1)S...) while((s32[]{:T(128)}, bf16[2048,64]{0,1:T(8,128)(2,1)S(1)}, ...), condition=%wide.region_12.13_spmd.clone, body=%wide.region_9.12_spmd.clone.sunk | while | flops 277939712 | bytes 17525440 | solution.py:88
  824.8 38.2 %reduce-scatter.5.cloned.1.call-done = bf16[512,768]{1,0:T(8,128)(2,1)} async-done(((bf16[2048,768]{1,0:T(8,128)(2,1)}), bf16[512,768]{1,0:T(8,128)(2,1)}) %reduce-scatter.5.cloned.1.call-update) | async-done | bytes 786448 | tf_op jit(solution)/shard_map/reduce_scatter | solution.py:220
  869.9 25.6 %all-gather.7.cloned.1.call-done = bf16[2048,768]{1,0:T(8,128)(2,1)} async-done(((bf16[512,768]{1,0:T(8,128)(2,1)}), bf16[2048,768]{1,0:T(8,128)(2,1)}) %all-gather.7.cloned.1.call-update) | async-done | bytes 3145744 | tf_op jit(solution)/shard_map/all_gather | solution.py:227
  909.7 38.0 %reduce-scatter.7.cloned.1.call-done = bf16[512,768]{1,0:T(8,128)(2,1)} async-done(((bf16[2048,768]{1,0:T(8,128)(2,1)}), bf16[512,768]{1,0:T(8,128)(2,1)}) %reduce-scatter.7.cloned.1.call-update) | async-done | bytes 786448 | tf_op jit(solution)/shard_map/reduce_scatter | solution.py:233
  950.5 28.6 %all-gather.9.cloned.1.call-done = bf16[2048,768]{1,0:T(8,128)(2,1)} async-done(((bf16[512,768]{1,0:T(8,128)(2,1)}), bf16[2048,768]{1,0:T(8,128)(2,1)}) %all-gather.9.cloned.1.call-update) | async-done | bytes 3145744 | tf_op jit(solution)/shard_map/all_gather | solution.py:243
  995.6 38.1 %reduce-scatter.9.cloned.1.call-done = bf16[512,768]{1,0:T(8,128)(2,1)} async-done(((bf16[2048,768]{1,0:T(8,128)(2,1)}), bf16[512,768]{1,0:T(8,128)(2,1)}) %reduce-scatter.9.cloned.1.call-update) | async-done | bytes 786448 | tf_op jit(solution)/shard_map/reduce_scatter | solution.py:260
  1038.9 28.6 %all-gather.11.cloned.1.call-done = bf16[2048,768]{1,0:T(8,128)(2,1)} async-done(((bf16[512,768]{1,0:T(8,128)(2,1)}), bf16[2048,768]{1,0:T(8,128)(2,1)}) %all-gather.11.cloned.1.call-update) | async-done | bytes 3145744 | tf_op jit(solution)/shard_map/all_gather | solution.py:271
  1080.0 76.9 %while.113 = (s32[]{:T(128)}, bf16[2048,64]{0,1:T(8,128)(2,1)}, f32[2048,64]{0,1:T(8,128)}, f32[2048,64]{0,1:T(8,128)S(1)}, f32[4,512,2048]{2,1,0:T(8,128)}, /*i...) while((s32[]{:T(128)}, bf16[2048,64]{0,1:T(8,128)(2,1)}, ...), condition=%wide.region_30.31_spmd.clone, body=%wide.region_28.30_spmd.clone.sunk | while | flops 684393984 | bytes 81214752 | solution.py:154
  1166.4 82.4 %while.112 = (s32[]{:T(128)}, bf16[2048,64]{0,1:T(8,128)(2,1)}, f32[2048,64]{0,1:T(8,128)}, f32[2048,64]{0,1:T(8,128)}, f32[4,512,2048]{2,1,0:T(8,128)}, /*index...) while((s32[]{:T(128)}, bf16[2048,64]{0,1:T(8,128)(2,1)}, ...), condition=%wide.region_27.28_spmd.clone, body=%wide.region_25.27_spmd.clone.sunk | while | flops 684393984 | bytes 80952608 | solution.py:154
  1257.5 77.5 %while.111 = (s32[]{:T(128)}, bf16[2048,64]{0,1:T(8,128)(2,1)}, f32[2048,64]{0,1:T(8,128)}, f32[2048,64]{0,1:T(8,128)}, f32[4,512,2048]{2,1,0:T(8,128)}, /*index...) while((s32[]{:T(128)}, bf16[2048,64]{0,1:T(8,128)(2,1)}, ...), condition=%wide.region_24.25_spmd.clone, body=%wide.region_22.24_spmd.clone.sunk | while | flops 684393984 | bytes 81214752 | solution.py:154
  1365.5 34.8 %pad_maximum_fusion.1 = f32[3,4,512,2048]{3,2,1,0:T(8,128)} fusion(f32[1,4,512,2048]{3,2,1,0:T(8,128)} %bitcast.176, f32[1,4,512,2048]{3,2,1,0:T(8,128)} %bitcast.177, f32[1,4,512,2048]{3,2,1,0:T(8,128)} %bitcast.175), kind=kLoop, calls=%fused_computation.121 | loop fusion | flops 25165824 | bytes 100663296 | tf_op jit(solution)/shard_map/stack | solution.py:305
  1400.3 32.0 %slice_bitcast_fusion.6 = (f32[3,512,2048]{2,1,0:T(8,128)}, f32[3,512,2048]{2,1,0:T(8,128)}, f32[3,512,2048]{2,1,0:T(8,128)}, f32[3,512,2048]{2,1,0:T(8,128)}) fusion(f32[3,4,512,2048]{3,2,1,0:T(8,128)} %pad_maximum_fusion.1), kind=kLoop, calls=%fused_computation.128 | loop fusion | bytes 100663296 | tf_op jit(solution)/shard_map/transpose(jvp())/unstack | solution.py:58
  1444.8 25.4 %reshape.276 = f32[3929088]{0:T(1024)} reshape(f32[3,512,2558]{2,1,0:T(8,128)} %pad.36) | data formatting | bytes 31432704
  1470.1 22.6 %reshape.234 = f32[3,1309696]{1,0:T(4,128)} reshape(f32[3929088]{0:T(1024)} %reshape.276) | data formatting | bytes 31432704 | tf_op jit(solution)/shard_map/transpose(jvp())/reshape | solution.py:48
  1510.0 47.6 %reshape.278 = f32[3938301]{0:T(1024)} reshape(f32[3,1312767]{1,0:T(4,128)} %pad.37) | data formatting | bytes 31506408
  1557.6 26.2 %reshape.235 = f32[3,513,2559]{2,1,0:T(8,128)} reshape(f32[3938301]{0:T(1024)} %reshape.278) | data formatting | bytes 31506408 | tf_op jit(solution)/shard_map/transpose(jvp())/reshape | solution.py:46
  1596.2 25.6 %reshape.272 = f32[3929088]{0:T(1024)} reshape(f32[3,512,2558]{2,1,0:T(8,128)} %pad.39) | data formatting | bytes 31432704
  1621.8 22.5 %reshape.236 = f32[3,1309696]{1,0:T(4,128)} reshape(f32[3929088]{0:T(1024)} %reshape.272) | data formatting | bytes 31432704 | tf_op jit(solution)/shard_map/transpose(jvp())/reshape | solution.py:48
  1661.0 46.3 %reshape.274 = f32[3938301]{0:T(1024)} reshape(f32[3,1312767]{1,0:T(4,128)} %pad.40) | data formatting | bytes 31506408
  1707.3 25.9 %reshape.237 = f32[3,513,2559]{2,1,0:T(8,128)} reshape(f32[3938301]{0:T(1024)} %reshape.274) | data formatting | bytes 31506408 | tf_op jit(solution)/shard_map/transpose(jvp())/reshape | solution.py:46
  1745.2 25.3 %reshape.268 = f32[3929088]{0:T(1024)} reshape(f32[3,512,2558]{2,1,0:T(8,128)} %pad.42) | data formatting | bytes 31432704
  1770.5 22.5 %reshape.238 = f32[3,1309696]{1,0:T(4,128)} reshape(f32[3929088]{0:T(1024)} %reshape.268) | data formatting | bytes 31432704 | tf_op jit(solution)/shard_map/transpose(jvp())/reshape | solution.py:48
  1809.8 46.5 %reshape.270 = f32[3938301]{0:T(1024)} reshape(f32[3,1312767]{1,0:T(4,128)} %pad.43) | data formatting | bytes 31506408
  1856.3 25.7 %reshape.239 = f32[3,513,2559]{2,1,0:T(8,128)} reshape(f32[3938301]{0:T(1024)} %reshape.270) | data formatting | bytes 31506408 | tf_op jit(solution)/shard_map/transpose(jvp())/reshape | solution.py:46
  1894.0 25.3 %reshape.264 = f32[3929088]{0:T(1024)} reshape(f32[3,512,2558]{2,1,0:T(8,128)} %pad.45) | data formatting | bytes 31432704
  1958.7 46.3 %reshape.266 = f32[3938301]{0:T(1024)} reshape(f32[3,1312767]{1,0:T(4,128)} %pad.46) | data formatting | bytes 31506408
  2005.0 25.6 %reshape.241 = f32[3,513,2559]{2,1,0:T(8,128)} reshape(f32[3938301]{0:T(1024)} %reshape.266) | data formatting | bytes 31506408 | tf_op jit(solution)/shard_map/transpose(jvp())/reshape | solution.py:46
  2077.4 44.5 %all-reduce.12 = (f32[]{:T(128)}, f32[]{:T(128)}, f32[768]{0:T(1024)S(1)}, f32[768]{0:T(1024)S(1)}) all-reduce(f32[]{:T(128)} %get-tuple-element.1419, f32[]{:T(128)} %fusion.150, f32[768]{0:T(1024)S(1)} %get-tuple-element.1420, f32[768]{0:T(1024)S(1)} %copy-done.64), channel_id=1, replica_groups=mesh['dp'=8,'tensor'=4] {'dp','tensor'}, use_global_device_ids=true, to_apply=%region_17.18 | all-reduce | flops 1538 | bytes 12304 | tf_op jit(solution)/shard_map/psum | solution.py:321
  (485 shorter events, 819.0 us)
Async XLA Ops:
  7.2 898.9 %copy-start = (bf16[512,768]{1,0:T(8,128)(2,1)S(1)}, bf16[512,768]{1,0:T(8,128)(2,1)}, u32[]{:S(2)}) copy-start(bf16[512,768]{1,0:T(8,128)(2,1)} %param.39) | copy-start | bytes 2359300
  7.2 696.0 %all-gather.5.cloned.1.call-start = ((), (), s32[]{:S(2)}) async-start(), calls=%async_computation.4 | async-start | bytes 3932160 | tf_op jit(solution)/shard_map/all_gather | solution.py:192
  12.8 850.2 %reduce-scatter.5.cloned.1.call-start = ((), (), s32[]{:S(2)}) async-start(), calls=%async_computation.5 | async-start | bytes 3932160 | tf_op jit(solution)/shard_map/reduce_scatter | solution.py:220
  429.5 24.8 %copy-start.46 = (f32[3,2559]{1,0:T(4,128)S(1)}, f32[3,2559]{1,0:T(4,128)}, u32[]{:S(2)}) copy-start(f32[3,2559]{1,0:T(4,128)} %get-tuple-element.1596) | copy-start | bytes 92128
  600.7 21.3 copy-start.15
  669.8 33.4 %copy-start.39 = (bf16[768,192]{0,1:T(8,128)(2,1)S(1)}, bf16[768,192]{0,1:T(8,128)(2,1)}, u32[]{:S(2)}) copy-start(bf16[768,192]{0,1:T(8,128)(2,1)} %param.31) | copy-start | bytes 884740
  820.7 42.3 %copy-start.13 = (bf16[512,768]{1,0:T(8,128)(2,1)S(1)}, bf16[512,768]{1,0:T(8,128)(2,1)}, u32[]{:S(2)}) copy-start(bf16[512,768]{1,0:T(8,128)(2,1)} %param.26) | copy-start | bytes 2359300
  824.7 70.8 %all-gather.7.cloned.1.call-start = ((), (), s32[]{:S(2)}) async-start(), calls=%async_computation.6 | async-start | bytes 3932160 | tf_op jit(solution)/shard_map/all_gather | solution.py:227
  824.8 42.1 %copy-start.37 = (bf16[768,512]{1,0:T(8,128)(2,1)S(1)}, bf16[768,512]{1,0:T(8,128)(2,1)}, u32[]{:S(2)}) copy-start(bf16[768,512]{1,0:T(8,128)(2,1)} %param.37) | copy-start | bytes 2359300
  824.8 212.2 %copy-start.47 = (f32[768]{0:T(1024)}, f32[768]{0:T(1024)S(1)}, u32[]{:S(2)}) copy-start(f32[768]{0:T(1024)S(1)} %convert_element_type.265) | copy-start | bytes 9220
  864.5 172.5 %copy-start.53 = (f32[512]{0:T(512)}, f32[512]{0:T(512)S(1)}, u32[]{:S(2)}) copy-start(f32[512]{0:T(512)S(1)} %fusion.149) | copy-start | bytes 6148
  866.8 80.9 %reduce-scatter.7.cloned.1.call-start = ((), (), s32[]{:S(2)}) async-start(), calls=%async_computation.7 | async-start | bytes 3932160 | tf_op jit(solution)/shard_map/reduce_scatter | solution.py:233
  906.1 41.7 %copy-start.16 = (bf16[512,768]{1,0:T(8,128)(2,1)S(1)}, bf16[512,768]{1,0:T(8,128)(2,1)}, u32[]{:S(2)}) copy-start(bf16[512,768]{1,0:T(8,128)(2,1)} %reduce-scatter.5.cloned.1.call-done) | copy-start | bytes 2359300
  909.6 69.5 %all-gather.9.cloned.1.call-start = ((), (), s32[]{:S(2)}) async-start(), calls=%async_computation.8 | async-start | bytes 3932160 | tf_op jit(solution)/shard_map/all_gather | solution.py:243
  909.7 127.3 %copy-start.51 = (f32[512]{0:T(512)}, f32[512]{0:T(512)S(1)}, u32[]{:S(2)}) copy-start(f32[512]{0:T(512)S(1)} %fusion.147) | copy-start | bytes 6148
  950.5 83.2 %reduce-scatter.9.cloned.1.call-start = ((), (), s32[]{:S(2)}) async-start(), calls=%async_computation.9 | async-start | bytes 3932160 | tf_op jit(solution)/shard_map/reduce_scatter | solution.py:260
  989.1 44.6 %copy-start.24 = (bf16[512,768]{1,0:T(8,128)(2,1)S(1)}, bf16[512,768]{1,0:T(8,128)(2,1)}, u32[]{:S(2)}) copy-start(bf16[512,768]{1,0:T(8,128)(2,1)} %param.27) | copy-start | bytes 2359300
  995.6 71.9 %copy-start.45 = (bf16[192,768]{1,0:T(8,128)(2,1)S(1)}, bf16[192,768]{1,0:T(8,128)(2,1)}, u32[]{:S(2)}) copy-start(bf16[192,768]{1,0:T(8,128)(2,1)} %param.34) | copy-start | bytes 884740
  995.6 71.9 %all-gather.11.cloned.1.call-start = ((), (), s32[]{:S(2)}) async-start(), calls=%async_computation.10 | async-start | bytes 3932160 | tf_op jit(solution)/shard_map/all_gather | solution.py:271
  1037.0 33.5 %copy-start.62 = (f32[512]{0:T(512)}, f32[512]{0:T(512)S(1)}, u32[]{:S(2)}) copy-start(f32[512]{0:T(512)S(1)} %multiply_multiply_fusion.4) | copy-start | bytes 6148
  1038.8 1036.6 %reduce-scatter.11.cloned.1.call-start = ((), (), s32[]{:S(2)}) async-start(), calls=%async_computation.11 | async-start | bytes 3932160 | tf_op jit(solution)/shard_map/reduce_scatter | solution.py:310
  1105.7 7.4 copy-start.2
  1144.2 7.3 copy-start.2
  1157.7 8.7 copy-start.12
  1157.7 8.7 copy-start.21
  1173.3 7.3 copy-start.4
  1214.0 7.4 copy-start.4
  1234.6 7.3 copy-start.4
  1248.8 8.7 copy-start.10
  1248.8 8.7 copy-start.19
  1301.7 7.4 copy-start.6
  1335.0 8.4 copy-start.23
  1335.0 9.9 copy-start.40
  1335.0 9.9 copy-start.42
  1335.1 9.9 copy-start.44
  1349.0 779.6 %all-reduce.16.cloned.1.call-start = ((), (), s32[]{:S(2)}) async-start(), calls=%async_computation.12 | async-start | bytes 14155776 | tf_op jit(solution)/shard_map/psum | solution.py:324
  2049.9 25.5 %copy-start.14 = (bf16[512,768]{1,0:T(8,128)(2,1)S(1)}, bf16[512,768]{1,0:T(8,128)(2,1)}, u32[]{:S(2)}) copy-start(bf16[512,768]{1,0:T(8,128)(2,1)} %param.26) | copy-start | bytes 2359300
  2049.9 25.5 %copy-start.50 = (f32[768]{0:T(1024)S(1)}, f32[768]{0:T(1024)}, u32[]{:S(2)}) copy-start(f32[768]{0:T(1024)} %copy-done.49) | copy-start | bytes 9220
  2049.9 25.5 %copy-start.57 = (f32[512]{0:T(512)S(1)}, f32[512]{0:T(512)}, u32[]{:S(2)}) copy-start(f32[512]{0:T(512)} %copy-done.56) | copy-start | bytes 6148
  2049.9 27.4 %copy-start.64 = (f32[768]{0:T(1024)S(1)}, f32[768]{0:T(1024)}, u32[]{:S(2)}) copy-start(f32[768]{0:T(1024)} %get-tuple-element.1417) | copy-start | bytes 9220
  2049.9 73.9 %copy-start.61 = (f32[512]{0:T(512)S(1)}, f32[512]{0:T(512)}, u32[]{:S(2)}) copy-start(f32[512]{0:T(512)} %copy-done.60) | copy-start | bytes 6148
  2049.9 75.1 %copy-start.17 = (bf16[512,768]{1,0:T(8,128)(2,1)S(1)}, bf16[512,768]{1,0:T(8,128)(2,1)}, u32[]{:S(2)}) copy-start(bf16[512,768]{1,0:T(8,128)(2,1)} %reduce-scatter.5.cloned.1.call-done) | copy-start | bytes 2359300
  2049.9 75.1 %copy-start.25 = (bf16[512,768]{1,0:T(8,128)(2,1)S(1)}, bf16[512,768]{1,0:T(8,128)(2,1)}, u32[]{:S(2)}) copy-start(bf16[512,768]{1,0:T(8,128)(2,1)} %param.27) | copy-start | bytes 2359300
  2050.0 75.1 %copy-start.27 = (bf16[512,768]{1,0:T(8,128)(2,1)S(1)}, bf16[512,768]{1,0:T(8,128)(2,1)}, u32[]{:S(2)}) copy-start(bf16[512,768]{1,0:T(8,128)(2,1)} %reduce-scatter.7.cloned.1.call-done) | copy-start | bytes 2359300
  2050.0 75.1 %copy-start.48 = (f32[768]{0:T(1024)S(1)}, f32[768]{0:T(1024)}, u32[]{:S(2)}) copy-start(f32[768]{0:T(1024)} %copy-done.47) | copy-start | bytes 9220
  2050.0 75.1 %copy-start.52 = (f32[512]{0:T(512)S(1)}, f32[512]{0:T(512)}, u32[]{:S(2)}) copy-start(f32[512]{0:T(512)} %copy-done.51) | copy-start | bytes 6148
  2050.0 75.1 %copy-start.54 = (f32[512]{0:T(512)S(1)}, f32[512]{0:T(512)}, u32[]{:S(2)}) copy-start(f32[512]{0:T(512)} %copy-done.53) | copy-start | bytes 6148
  2050.0 75.1 %copy-start.63 = (f32[512]{0:T(512)S(1)}, f32[512]{0:T(512)}, u32[]{:S(2)}) copy-start(f32[512]{0:T(512)} %copy-done.62) | copy-start | bytes 6148
  (51 other events, 213.0 us)
Sparse Core Ops, SparseCore 0:
  12.9 28.7 all-gather.4
  824.8 38.1 reduce-scatter.4
  866.9 28.5 all-gather.6
  909.8 37.9 reduce-scatter.6
  950.6 28.5 all-gather.8
  995.7 37.9 reduce-scatter.8
  1038.9 28.5 all-gather.10
  1349.2 37.9 reduce-scatter.10
  1392.8 235.1 all-reduce.15
where the time goes:
time: 2160 us; the launch traced here: 2140 us
  local copies, waits for them, and re-layouts  1340 us (62%)
  matrix products  269 us (12%)
  other arithmetic  252 us (12%)
  waiting for transfers between devices  197 us (9%)
  blocking collectives  62.7 us (3%)
    unnamed x163, local copies, waits for them, and re-layouts  585 us
    reshape x8, local copies, waits for them, and re-layouts, band_matrix(): return tiled.reshape(heads_here, block_rows, span - 1)[:, :, :seq_len]  189 us
    another operation x8, local copies, waits for them, and re-layouts, band_matrix(): tiled = jnp.tile(window, (1, block_rows + 1))  126 us
    reshape x4, local copies, waits for them, and re-layouts, band_matrix(): tiled = jnp.tile(window, (1, block_rows + 1))  103 us
    dynamic_update_slice x12, other arithmetic, one_block(): lax.dynamic_update_slice_in_dim(grad_band, current + grad_scores.astype(j...  88.1 us
    slice x4, local copies, waits for them, and re-layouts, band_matrix(): tiled = tiled[:, block_rows - 1:block_rows - 1 + block_rows * (span - 1)]  86.8 us
    dot_general x24, matrix products, one_block(): lax.dot_general(query_block, key_head, contract_cols, preferred_element_t...  84 us
    pad x4, local copies, waits for them, and re-layouts, band_matrix(): tiled = tiled[:, block_rows - 1:block_rows - 1 + block_rows * (span - 1)]  67.5 us
  transfers between devices with their start and end apart: 9, of which 6 were waited for; matrix products, arithmetic and copies ran while one was open for 66% of the time, Pallas kernels for 0%

commit v1 on v0

--- a/solution.py
+++ b/solution.py
@@ -10,6 +10,11 @@
 contract_rows = (((0,), (0,)), ((), ()))
 contract_cols = (((1,), (1,)), ((), ()))
 contract_table = (((0,), (1,)), ((), ()))
+
+
+def axis_by_axis(x, one, other):
+    partial = lax.psum(x, one)
+    return lax.psum(partial, other)
 
 
 def row_norm(values, gain):
@@ -318,8 +323,8 @@
     _, norm_back_attn = jax.vjp(row_norm, source, gain_a)
     grad_source_part, grad_gain_attn = norm_back_attn(grad_normed)
     grad_source = grad_middle + grad_source_part
-    gain_attn_total, gain_ff_total, loss_total, count_total = lax.psum(
-        (grad_gain_attn, grad_gain_ff, loss_part, count_part), ("dp", "tensor")
+    gain_attn_total, gain_ff_total, loss_total, count_total = axis_by_axis(
+        (grad_gain_attn, grad_gain_ff, loss_part, count_part), "dp", "tensor"
     )
     grad_w_joint, grad_out, grad_table, grad_w_pair, grad_down = lax.psum(
         (grad_w_joint, grad_out, grad_table, grad_w_pair, grad_down), "dp"

time: 2160 us -> 2140 us (level)
  blocking collectives: 62.7 us -> 41 us
    psum x2, blocking collectives: 62.7 us -> 41 us  [the longest x1 33.9 us: axis_by_axis(): partial = lax.psum(x, one)]
where the time goes in v1:
time: 2140 us; the launch traced here: 2120 us
  local copies, waits for them, and re-layouts  1340 us (63%)
  matrix products  269 us (13%)
  other arithmetic  251 us (12%)
  waiting for transfers between devices  197 us (9%)
  blocking collectives  41 us (2%)
    unnamed x163, local copies, waits for them, and re-layouts  585 us
    reshape x8, local copies, waits for them, and re-layouts, band_matrix(): return tiled.reshape(heads_here, block_rows, span - 1)[:, :, :seq_len]  189 us
    another operation x8, local copies, waits for them, and re-layouts, band_matrix(): tiled = jnp.tile(window, (1, block_rows + 1))  126 us
    reshape x4, local copies, waits for them, and re-layouts, band_matrix(): tiled = jnp.tile(window, (1, block_rows + 1))  103 us
    dynamic_update_slice x12, other arithmetic, one_block(): lax.dynamic_update_slice_in_dim(grad_band, current + grad_scores.astype(j...  88.1 us
    slice x4, local copies, waits for them, and re-layouts, band_matrix(): tiled = tiled[:, block_rows - 1:block_rows - 1 + block_rows * (span - 1)]  86.8 us
    dot_general x24, matrix products, one_block(): lax.dot_general(query_block, key_head, contract_cols, preferred_element_t...  84 us
    pad x4, local copies, waits for them, and re-layouts, band_matrix(): tiled = tiled[:, block_rows - 1:block_rows - 1 + block_rows * (span - 1)]  67.5 us
  transfers between devices with their start and end apart: 9, of which 6 were waited for; matrix products, arithmetic and copies ran while one was open for 66% of the time, Pallas kernels for 0%

profile of v1, /device:TPU:12, one launch (start us, length us, event | category | flops | bytes accessed | tf_op | source)
XLA Modules:
  0.0 2122.2 jit_solution(13337127635505050100)
XLA Ops:
  22.7 24.2 %reshape.252 = f32[3938301]{0:T(1024)} reshape(f32[3,513,2559]{2,1,0:T(8,128)} %tile.40) | data formatting | bytes 31506408
  46.9 23.7 %tile.41 = f32[3,1312767]{1,0:T(4,128)} reshape(f32[3938301]{0:T(1024)} %reshape.252) | data formatting | bytes 31506408 | tf_op jit(solution)/shard_map/tile | solution.py:51
  92.4 44.4 %reshape.254 = f32[3929088]{0:T(1024)} reshape(f32[3,1309696]{1,0:T(4,128)} %slice.146) | data formatting | bytes 31432704
  136.9 24.7 %reshape.232 = f32[3,512,2558]{2,1,0:T(8,128)} reshape(f32[3929088]{0:T(1024)} %reshape.254) | data formatting | bytes 31432704 | tf_op jit(solution)/shard_map/reshape | solution.py:53
  169.1 24.2 %reshape.248 = f32[3938301]{0:T(1024)} reshape(f32[3,513,2559]{2,1,0:T(8,128)} %tile.42) | data formatting | bytes 31506408
  193.3 23.7 %tile.43 = f32[3,1312767]{1,0:T(4,128)} reshape(f32[3938301]{0:T(1024)} %reshape.248) | data formatting | bytes 31506408 | tf_op jit(solution)/shard_map/tile | solution.py:51
  238.6 44.6 %reshape.250 = f32[3929088]{0:T(1024)} reshape(f32[3,1309696]{1,0:T(4,128)} %slice.149) | data formatting | bytes 31432704
  283.2 24.8 %reshape.233 = f32[3,512,2558]{2,1,0:T(8,128)} reshape(f32[3929088]{0:T(1024)} %reshape.250) | data formatting | bytes 31432704 | tf_op jit(solution)/shard_map/reshape | solution.py:53
  315.6 23.9 %reshape.260 = f32[3938301]{0:T(1024)} reshape(f32[3,513,2559]{2,1,0:T(8,128)} %tile.16) | data formatting | bytes 31506408
  339.5 23.7 %tile.17 = f32[3,1312767]{1,0:T(4,128)} reshape(f32[3938301]{0:T(1024)} %reshape.260) | data formatting | bytes 31506408 | tf_op jit(solution)/shard_map/tile | solution.py:51
  385.1 44.4 %reshape.262 = f32[3929088]{0:T(1024)} reshape(f32[3,1309696]{1,0:T(4,128)} %slice.140) | data formatting | bytes 31432704
  429.5 24.8 %reshape.230 = f32[3,512,2558]{2,1,0:T(8,128)} reshape(f32[3929088]{0:T(1024)} %reshape.262) | data formatting | bytes 31432704 | tf_op jit(solution)/shard_map/reshape | solution.py:53
  461.8 24.2 %reshape.256 = f32[3938301]{0:T(1024)} reshape(f32[3,513,2559]{2,1,0:T(8,128)} %tile.18) | data formatting | bytes 31506408
  486.0 23.7 %tile.19 = f32[3,1312767]{1,0:T(4,128)} reshape(f32[3938301]{0:T(1024)} %reshape.256) | data formatting | bytes 31506408 | tf_op jit(solution)/shard_map/tile | solution.py:51
  531.3 44.7 %reshape.258 = f32[3929088]{0:T(1024)} reshape(f32[3,1309696]{1,0:T(4,128)} %slice.143) | data formatting | bytes 31432704
  576.0 24.8 %reshape.231 = f32[3,512,2558]{2,1,0:T(8,128)} reshape(f32[3929088]{0:T(1024)} %reshape.258) | data formatting | bytes 31432704 | tf_op jit(solution)/shard_map/reshape | solution.py:53
  635.4 34.5 %pad_maximum_fusion = f32[3,4,512,2048]{3,2,1,0:T(8,128)} fusion(f32[3,1,512,2048]{3,2,1,0:T(8,128)} %get-tuple-element.1602, f32[3,1,512,2048]{3,2,1,0:T(8,128)} %get-tuple-element.1603, f32[3,1,512,2048]{3,2,1,0:T(8,128)} %get-tuple-element.1604, f32[3,1,512,2048]{3,2,1,0:T(8,128)} %get-tuple-element.1605), kind=kLoop, calls=%fused_computation.120 | loop fusion | flops 37748736 | bytes 100663296 | tf_op jit(solution)/shard_map/stack | solution.py:63
  669.9 33.4 %slice_bitcast_fusion = (f32[4,512,2048]{2,1,0:T(8,128)}, f32[4,512,2048]{2,1,0:T(8,128)}, f32[4,512,2048]{2,1,0:T(8,128)}) fusion(f32[3,4,512,2048]{3,2,1,0:T(8,128)} %pad_maximum_fusion), kind=kLoop, calls=%fused_computation.122 | loop fusion | bytes 100663296 | tf_op jit(solution)/shard_map/squeeze | solution.py:217
  715.1 31.0 %while.109 = (s32[]{:T(128)}, bf16[2048,64]{0,1:T(8,128)(2,1)}, f32[2048]{0:T(1024)}, bf16[2048,64]{1,0:T(8,128)(2,1)}, bf16[2048,64]{1,0:T(8,128)(2,1)S(1)}, /*...) while((s32[]{:T(128)}, bf16[2048,64]{0,1:T(8,128)(2,1)}, ...), condition=%wide.region_8.9_spmd.clone, body=%wide.region_5.8_spmd.clone.sunk | while | flops 277939712 | bytes 17525440 | solution.py:93
  756.9 23.2 %while.108 = (s32[]{:T(128)}, bf16[2048,64]{0,1:T(8,128)(2,1)S(1)}, f32[2048]{0:T(1024)S(1)}, bf16[2048,64]{1,0:T(8,128)(2,1)}, bf16[2048,64]{1,0:T(8,128)(2,1)S...) while((s32[]{:T(128)}, bf16[2048,64]{0,1:T(8,128)(2,1)S(1)}, ...), condition=%wide.region_4.5_spmd.clone, body=%wide.region_1.4_spmd.clone.sunk | while | flops 277939712 | bytes 17787584 | solution.py:93
  792.3 27.5 %while.110 = (s32[]{:T(128)}, bf16[2048,64]{0,1:T(8,128)(2,1)S(1)}, f32[2048]{0:T(1024)S(1)}, bf16[2048,64]{1,0:T(8,128)(2,1)}, bf16[2048,64]{1,0:T(8,128)(2,1)S...) while((s32[]{:T(128)}, bf16[2048,64]{0,1:T(8,128)(2,1)S(1)}, ...), condition=%wide.region_12.13_spmd.clone, body=%wide.region_9.12_spmd.clone.sunk | while | flops 277939712 | bytes 17525440 | solution.py:93
  824.9 38.2 %reduce-scatter.5.cloned.1.call-done = bf16[512,768]{1,0:T(8,128)(2,1)} async-done(((bf16[2048,768]{1,0:T(8,128)(2,1)}), bf16[512,768]{1,0:T(8,128)(2,1)}) %reduce-scatter.5.cloned.1.call-update) | async-done | bytes 786448 | tf_op jit(solution)/shard_map/reduce_scatter | solution.py:225
  870.0 25.6 %all-gather.7.cloned.1.call-done = bf16[2048,768]{1,0:T(8,128)(2,1)} async-done(((bf16[512,768]{1,0:T(8,128)(2,1)}), bf16[2048,768]{1,0:T(8,128)(2,1)}) %all-gather.7.cloned.1.call-update) | async-done | bytes 3145744 | tf_op jit(solution)/shard_map/all_gather | solution.py:232
  909.8 38.0 %reduce-scatter.7.cloned.1.call-done = bf16[512,768]{1,0:T(8,128)(2,1)} async-done(((bf16[2048,768]{1,0:T(8,128)(2,1)}), bf16[512,768]{1,0:T(8,128)(2,1)}) %reduce-scatter.7.cloned.1.call-update) | async-done | bytes 786448 | tf_op jit(solution)/shard_map/reduce_scatter | solution.py:238
  950.6 28.6 %all-gather.9.cloned.1.call-done = bf16[2048,768]{1,0:T(8,128)(2,1)} async-done(((bf16[512,768]{1,0:T(8,128)(2,1)}), bf16[2048,768]{1,0:T(8,128)(2,1)}) %all-gather.9.cloned.1.call-update) | async-done | bytes 3145744 | tf_op jit(solution)/shard_map/all_gather | solution.py:248
  995.7 38.1 %reduce-scatter.9.cloned.1.call-done = bf16[512,768]{1,0:T(8,128)(2,1)} async-done(((bf16[2048,768]{1,0:T(8,128)(2,1)}), bf16[512,768]{1,0:T(8,128)(2,1)}) %reduce-scatter.9.cloned.1.call-update) | async-done | bytes 786448 | tf_op jit(solution)/shard_map/reduce_scatter | solution.py:265
  1039.0 28.6 %all-gather.11.cloned.1.call-done = bf16[2048,768]{1,0:T(8,128)(2,1)} async-done(((bf16[512,768]{1,0:T(8,128)(2,1)}), bf16[2048,768]{1,0:T(8,128)(2,1)}) %all-gather.11.cloned.1.call-update) | async-done | bytes 3145744 | tf_op jit(solution)/shard_map/all_gather | solution.py:276
  1080.1 77.0 %while.113 = (s32[]{:T(128)}, bf16[2048,64]{0,1:T(8,128)(2,1)}, f32[2048,64]{0,1:T(8,128)}, f32[2048,64]{0,1:T(8,128)S(1)}, f32[4,512,2048]{2,1,0:T(8,128)}, /*i...) while((s32[]{:T(128)}, bf16[2048,64]{0,1:T(8,128)(2,1)}, ...), condition=%wide.region_32.33_spmd.clone, body=%wide.region_30.32_spmd.clone.sunk | while | flops 684393984 | bytes 81214752 | solution.py:159
  1166.6 82.4 %while.112 = (s32[]{:T(128)}, bf16[2048,64]{0,1:T(8,128)(2,1)}, f32[2048,64]{0,1:T(8,128)}, f32[2048,64]{0,1:T(8,128)}, f32[4,512,2048]{2,1,0:T(8,128)}, /*index...) while((s32[]{:T(128)}, bf16[2048,64]{0,1:T(8,128)(2,1)}, ...), condition=%wide.region_29.30_spmd.clone, body=%wide.region_27.29_spmd.clone.sunk | while | flops 684393984 | bytes 80952608 | solution.py:159
  1257.7 77.6 %while.111 = (s32[]{:T(128)}, bf16[2048,64]{0,1:T(8,128)(2,1)}, f32[2048,64]{0,1:T(8,128)}, f32[2048,64]{0,1:T(8,128)}, f32[4,512,2048]{2,1,0:T(8,128)}, /*index...) while((s32[]{:T(128)}, bf16[2048,64]{0,1:T(8,128)(2,1)}, ...), condition=%wide.region_26.27_spmd.clone, body=%wide.region_24.26_spmd.clone.sunk | while | flops 684393984 | bytes 81214752 | solution.py:159
  1365.7 34.6 %pad_maximum_fusion.1 = f32[3,4,512,2048]{3,2,1,0:T(8,128)} fusion(f32[1,4,512,2048]{3,2,1,0:T(8,128)} %bitcast.176, f32[1,4,512,2048]{3,2,1,0:T(8,128)} %bitcast.177, f32[1,4,512,2048]{3,2,1,0:T(8,128)} %bitcast.175), kind=kLoop, calls=%fused_computation.121 | loop fusion | flops 25165824 | bytes 100663296 | tf_op jit(solution)/shard_map/stack | solution.py:310
  1400.4 32.0 %slice_bitcast_fusion.6 = (f32[3,512,2048]{2,1,0:T(8,128)}, f32[3,512,2048]{2,1,0:T(8,128)}, f32[3,512,2048]{2,1,0:T(8,128)}, f32[3,512,2048]{2,1,0:T(8,128)}) fusion(f32[3,4,512,2048]{3,2,1,0:T(8,128)} %pad_maximum_fusion.1), kind=kLoop, calls=%fused_computation.128 | loop fusion | bytes 100663296 | tf_op jit(solution)/shard_map/transpose(jvp())/unstack | solution.py:63
  1444.8 25.4 %reshape.276 = f32[3929088]{0:T(1024)} reshape(f32[3,512,2558]{2,1,0:T(8,128)} %pad.36) | data formatting | bytes 31432704
  1470.2 22.6 %reshape.234 = f32[3,1309696]{1,0:T(4,128)} reshape(f32[3929088]{0:T(1024)} %reshape.276) | data formatting | bytes 31432704 | tf_op jit(solution)/shard_map/transpose(jvp())/reshape | solution.py:53
  1510.1 47.7 %reshape.278 = f32[3938301]{0:T(1024)} reshape(f32[3,1312767]{1,0:T(4,128)} %pad.37) | data formatting | bytes 31506408
  1557.7 26.2 %reshape.235 = f32[3,513,2559]{2,1,0:T(8,128)} reshape(f32[3938301]{0:T(1024)} %reshape.278) | data formatting | bytes 31506408 | tf_op jit(solution)/shard_map/transpose(jvp())/reshape | solution.py:51
  1596.3 25.6 %reshape.272 = f32[3929088]{0:T(1024)} reshape(f32[3,512,2558]{2,1,0:T(8,128)} %pad.39) | data formatting | bytes 31432704
  1621.9 22.6 %reshape.236 = f32[3,1309696]{1,0:T(4,128)} reshape(f32[3929088]{0:T(1024)} %reshape.272) | data formatting | bytes 31432704 | tf_op jit(solution)/shard_map/transpose(jvp())/reshape | solution.py:53
  1661.1 46.3 %reshape.274 = f32[3938301]{0:T(1024)} reshape(f32[3,1312767]{1,0:T(4,128)} %pad.40) | data formatting | bytes 31506408
  1707.5 25.9 %reshape.237 = f32[3,513,2559]{2,1,0:T(8,128)} reshape(f32[3938301]{0:T(1024)} %reshape.274) | data formatting | bytes 31506408 | tf_op jit(solution)/shard_map/transpose(jvp())/reshape | solution.py:51
  1745.3 25.3 %reshape.268 = f32[3929088]{0:T(1024)} reshape(f32[3,512,2558]{2,1,0:T(8,128)} %pad.42) | data formatting | bytes 31432704
  1809.9 46.5 %reshape.270 = f32[3938301]{0:T(1024)} reshape(f32[3,1312767]{1,0:T(4,128)} %pad.43) | data formatting | bytes 31506408
  1856.5 25.7 %reshape.239 = f32[3,513,2559]{2,1,0:T(8,128)} reshape(f32[3938301]{0:T(1024)} %reshape.270) | data formatting | bytes 31506408 | tf_op jit(solution)/shard_map/transpose(jvp())/reshape | solution.py:51
  1894.2 25.2 %reshape.264 = f32[3929088]{0:T(1024)} reshape(f32[3,512,2558]{2,1,0:T(8,128)} %pad.45) | data formatting | bytes 31432704
  1919.4 22.6 %reshape.240 = f32[3,1309696]{1,0:T(4,128)} reshape(f32[3929088]{0:T(1024)} %reshape.264) | data formatting | bytes 31432704 | tf_op jit(solution)/shard_map/transpose(jvp())/reshape | solution.py:53
  1958.9 46.3 %reshape.266 = f32[3938301]{0:T(1024)} reshape(f32[3,1312767]{1,0:T(4,128)} %pad.46) | data formatting | bytes 31506408
  2005.2 25.6 %reshape.241 = f32[3,513,2559]{2,1,0:T(8,128)} reshape(f32[3938301]{0:T(1024)} %reshape.266) | data formatting | bytes 31506408 | tf_op jit(solution)/shard_map/transpose(jvp())/reshape | solution.py:51
  2059.4 33.9 %all-reduce.12 = (f32[]{:T(128)}, f32[]{:T(128)}, f32[768]{0:T(1024)S(1)}, f32[32,3]{0,1:T(4,128)S(1)}, f32[768]{0:T(1024)S(1)}) all-reduce(f32[]{:T(128)} %get-tuple-element.1419, f32[]{:T(128)} %fusion.150, f32[768]{0:T(1024)S(1)} %get-tuple-element.1420, f32[32,3]{0,1:T(4,128)S(1)} %fusion.115, ...), channel_id=1, replica_groups=mesh['dp'=8,'tensor'=4] {'dp'}, use_global_device_ids=true, to_apply=%region_17.18 | all-reduce | flops 1634 | bytes 13072 | tf_op jit(solution)/shard_map/psum | solution.py:16
  (485 shorter events, 808.1 us)
Async XLA Ops:
  7.2 899.0 %copy-start = (bf16[512,768]{1,0:T(8,128)(2,1)S(1)}, bf16[512,768]{1,0:T(8,128)(2,1)}, u32[]{:S(2)}) copy-start(bf16[512,768]{1,0:T(8,128)(2,1)} %param.39) | copy-start | bytes 2359300
  7.2 696.1 %all-gather.5.cloned.1.call-start = ((), (), s32[]{:S(2)}) async-start(), calls=%async_computation.4 | async-start | bytes 3932160 | tf_op jit(solution)/shard_map/all_gather | solution.py:197
  12.8 850.3 %reduce-scatter.5.cloned.1.call-start = ((), (), s32[]{:S(2)}) async-start(), calls=%async_computation.5 | async-start | bytes 3932160 | tf_op jit(solution)/shard_map/reduce_scatter | solution.py:225
  429.5 24.8 %copy-start.46 = (f32[3,2559]{1,0:T(4,128)S(1)}, f32[3,2559]{1,0:T(4,128)}, u32[]{:S(2)}) copy-start(f32[3,2559]{1,0:T(4,128)} %get-tuple-element.1601) | copy-start | bytes 92128
  600.8 21.3 %copy-start.15 = (f32[3,512,2558]{2,1,0:T(8,128)S(1)}, f32[3,512,2558]{2,1,0:T(8,128)}, u32[]{:S(2)}) copy-start(f32[3,512,2558]{2,1,0:T(8,128)} %reshape.231) | copy-start | bytes 47149060
  669.9 33.4 %copy-start.39 = (bf16[768,192]{0,1:T(8,128)(2,1)S(1)}, bf16[768,192]{0,1:T(8,128)(2,1)}, u32[]{:S(2)}) copy-start(bf16[768,192]{0,1:T(8,128)(2,1)} %param.31) | copy-start | bytes 884740
  820.8 42.3 %copy-start.13 = (bf16[512,768]{1,0:T(8,128)(2,1)S(1)}, bf16[512,768]{1,0:T(8,128)(2,1)}, u32[]{:S(2)}) copy-start(bf16[512,768]{1,0:T(8,128)(2,1)} %param.26) | copy-start | bytes 2359300
  824.8 70.8 %all-gather.7.cloned.1.call-start = ((), (), s32[]{:S(2)}) async-start(), calls=%async_computation.6 | async-start | bytes 3932160 | tf_op jit(solution)/shard_map/all_gather | solution.py:232
  824.8 42.1 %copy-start.37 = (bf16[768,512]{1,0:T(8,128)(2,1)S(1)}, bf16[768,512]{1,0:T(8,128)(2,1)}, u32[]{:S(2)}) copy-start(bf16[768,512]{1,0:T(8,128)(2,1)} %param.37) | copy-start | bytes 2359300
  824.9 212.2 %copy-start.47 = (f32[768]{0:T(1024)}, f32[768]{0:T(1024)S(1)}, u32[]{:S(2)}) copy-start(f32[768]{0:T(1024)S(1)} %convert_element_type.265) | copy-start | bytes 9220
  864.6 172.6 %copy-start.53 = (f32[512]{0:T(512)}, f32[512]{0:T(512)S(1)}, u32[]{:S(2)}) copy-start(f32[512]{0:T(512)S(1)} %fusion.149) | copy-start | bytes 6148
  866.9 80.9 %reduce-scatter.7.cloned.1.call-start = ((), (), s32[]{:S(2)}) async-start(), calls=%async_computation.7 | async-start | bytes 3932160 | tf_op jit(solution)/shard_map/reduce_scatter | solution.py:238
  906.2 41.7 %copy-start.16 = (bf16[512,768]{1,0:T(8,128)(2,1)S(1)}, bf16[512,768]{1,0:T(8,128)(2,1)}, u32[]{:S(2)}) copy-start(bf16[512,768]{1,0:T(8,128)(2,1)} %reduce-scatter.5.cloned.1.call-done) | copy-start | bytes 2359300
  909.7 69.5 %all-gather.9.cloned.1.call-start = ((), (), s32[]{:S(2)}) async-start(), calls=%async_computation.8 | async-start | bytes 3932160 | tf_op jit(solution)/shard_map/all_gather | solution.py:248
  909.8 127.3 %copy-start.51 = (f32[512]{0:T(512)}, f32[512]{0:T(512)S(1)}, u32[]{:S(2)}) copy-start(f32[512]{0:T(512)S(1)} %fusion.147) | copy-start | bytes 6148
  950.6 83.2 %reduce-scatter.9.cloned.1.call-start = ((), (), s32[]{:S(2)}) async-start(), calls=%async_computation.9 | async-start | bytes 3932160 | tf_op jit(solution)/shard_map/reduce_scatter | solution.py:265
  989.2 44.6 %copy-start.24 = (bf16[512,768]{1,0:T(8,128)(2,1)S(1)}, bf16[512,768]{1,0:T(8,128)(2,1)}, u32[]{:S(2)}) copy-start(bf16[512,768]{1,0:T(8,128)(2,1)} %param.27) | copy-start | bytes 2359300
  995.7 71.9 %copy-start.45 = (bf16[192,768]{1,0:T(8,128)(2,1)S(1)}, bf16[192,768]{1,0:T(8,128)(2,1)}, u32[]{:S(2)}) copy-start(bf16[192,768]{1,0:T(8,128)(2,1)} %param.34) | copy-start | bytes 884740
  995.7 71.9 %all-gather.11.cloned.1.call-start = ((), (), s32[]{:S(2)}) async-start(), calls=%async_computation.10 | async-start | bytes 3932160 | tf_op jit(solution)/shard_map/all_gather | solution.py:276
  1037.1 33.5 %copy-start.62 = (f32[512]{0:T(512)}, f32[512]{0:T(512)S(1)}, u32[]{:S(2)}) copy-start(f32[512]{0:T(512)S(1)} %multiply_multiply_fusion.4) | copy-start | bytes 6148
  1038.9 1018.6 %reduce-scatter.11.cloned.1.call-start = ((), (), s32[]{:S(2)}) async-start(), calls=%async_computation.11 | async-start | bytes 3932160 | tf_op jit(solution)/shard_map/reduce_scatter | solution.py:315
  1105.8 7.4 copy-start.2
  1144.3 7.3 copy-start.2
  1157.9 8.7 copy-start.12
  1157.9 8.7 copy-start.21
  1193.6 7.3 copy-start.4
  1214.1 7.4 copy-start.4
  1234.8 7.4 copy-start.4
  1249.0 8.7 copy-start.10
  1249.0 8.7 copy-start.19
  1301.8 7.4 copy-start.6
  1335.2 8.4 copy-start.23
  1335.2 9.9 copy-start.40
  1335.3 9.9 copy-start.42
  1335.3 9.9 copy-start.44
  1349.2 758.0 %all-reduce.17.cloned.1.call-start = ((), (), s32[]{:S(2)}) async-start(), calls=%async_computation.12 | async-start | bytes 14155776 | tf_op jit(solution)/shard_map/psum | solution.py:329
  2050.1 7.4 copy-start.14
  2050.1 7.4 copy-start.50
  2050.1 7.4 copy-start.57
  2050.1 9.3 copy-start.64
  2050.2 52.2 %copy-start.61 = (f32[512]{0:T(512)S(1)}, f32[512]{0:T(512)}, u32[]{:S(2)}) copy-start(f32[512]{0:T(512)} %copy-done.60) | copy-start | bytes 6148
  2050.2 53.4 %copy-start.17 = (bf16[512,768]{1,0:T(8,128)(2,1)S(1)}, bf16[512,768]{1,0:T(8,128)(2,1)}, u32[]{:S(2)}) copy-start(bf16[512,768]{1,0:T(8,128)(2,1)} %reduce-scatter.5.cloned.1.call-done) | copy-start | bytes 2359300
  2050.2 53.4 %copy-start.25 = (bf16[512,768]{1,0:T(8,128)(2,1)S(1)}, bf16[512,768]{1,0:T(8,128)(2,1)}, u32[]{:S(2)}) copy-start(bf16[512,768]{1,0:T(8,128)(2,1)} %param.27) | copy-start | bytes 2359300
  2050.2 53.4 %copy-start.27 = (bf16[512,768]{1,0:T(8,128)(2,1)S(1)}, bf16[512,768]{1,0:T(8,128)(2,1)}, u32[]{:S(2)}) copy-start(bf16[512,768]{1,0:T(8,128)(2,1)} %reduce-scatter.7.cloned.1.call-done) | copy-start | bytes 2359300
  2050.2 53.4 %copy-start.48 = (f32[768]{0:T(1024)S(1)}, f32[768]{0:T(1024)}, u32[]{:S(2)}) copy-start(f32[768]{0:T(1024)} %copy-done.47) | copy-start | bytes 9220
  2050.2 53.4 %copy-start.52 = (f32[512]{0:T(512)S(1)}, f32[512]{0:T(512)}, u32[]{:S(2)}) copy-start(f32[512]{0:T(512)} %copy-done.51) | copy-start | bytes 6148
  2050.2 53.4 %copy-start.54 = (f32[512]{0:T(512)S(1)}, f32[512]{0:T(512)}, u32[]{:S(2)}) copy-start(f32[512]{0:T(512)} %copy-done.53) | copy-start | bytes 6148
  2050.2 53.4 %copy-start.63 = (f32[512]{0:T(512)S(1)}, f32[512]{0:T(512)}, u32[]{:S(2)}) copy-start(f32[512]{0:T(512)} %copy-done.62) | copy-start | bytes 6148
  (51 other events, 213.1 us)
Sparse Core Ops, SparseCore 0:
  12.9 28.7 all-gather.4
  824.9 38.1 reduce-scatter.4
  867.0 28.5 all-gather.6
  909.8 37.9 reduce-scatter.6
  950.7 28.5 all-gather.8
  995.8 37.9 reduce-scatter.8
  1039.0 28.5 all-gather.10
  1349.3 37.9 reduce-scatter.10
  1392.9 235.1 all-reduce.16
